TPU v7x, 32 devices: a whole 2x2x4 slice. The times are simulated.
32 devices in a mesh: groups: 2 (over y), slab: 16 (over z, x, core).
Axes of the slice: x: 2, y: 2, z: 4, core: 2. Of those that a mesh axis runs over, the one named last changes fastest.
Arguments:
- rhs: float32 [2, 64, 128, 128], P('groups', 'slab'), parts along dimension 0, may hold values from -6 to 6
- labels: int32 [64, 256, 128], P('slab', 'groups'), parts along dimension 1, may hold values from 0 to 4, as said below
- sigma_table: float32 [5, 3], replicated, may hold values from 0.05 to 2
Outputs:
- correction: float32 [2, 64, 128, 128], P('groups', 'slab'), parts along dimension 0
There are 2 independent parts, one for each index of `groups`. A program takes and returns all parts, laid end to end along the dimension named above; an argument that names none is the same for every part. Nothing has to cross between parts.
Inputs may be any that keep to these rules, and one draw needn't show every extreme that they name: Label 0 marks exactly the voxels outside an ellipsoid centred on the grid with semi-axes 0.45 * 128, 0.45 * 128 and 0.55 * 64 cells; inside, labels 1 to 4 are drawn independently for each voxel.
All inputs are finite; a program needn't handle non-finite values.
Results may differ from a plain program's by a relative error of at most 0.0002.
Values sent between devices are 32-bit elements; how exact they have to be, the bound alone decides.
A program may use at most 64 MiB of HBM per device.

v0:
```python
import jax
import jax.numpy as jnp
from jax import lax
from jax.sharding import PartitionSpec as P

LABELS = 5


OMEGA = 0.8


def extended_2(shard, sides, width):
    for axis, dim in sides:
        size, length = (lax.axis_size(axis), shard.shape[dim])
        up = [(i, (i + 1) % size) for i in range(size - 1)]
        down = [(j, i) for i, j in up]
        last = lax.slice_in_dim(shard, length - width, length, axis=dim)
        first = lax.slice_in_dim(shard, 0, width, axis=dim)
        before = lax.ppermute(last, axis, up)
        after = lax.ppermute(first, axis, down)
        shard = jnp.concatenate([before, shard, after], axis=dim)
    return shard


def harmonic(lower_side, upper_side):
    return 2.0 * lower_side * upper_side / (lower_side + upper_side)


def conductivity(padded, sigma_table, column):
    running = jnp.zeros(padded.shape, jnp.float32)
    for tissue in range(LABELS):
        running = running + jnp.where(padded == tissue, sigma_table[tissue, column], 0.0)
    return running


def coefficients(labels_ext, sigma_table):
    padded = jnp.pad(labels_ext, ((0, 0), (1, 1), (1, 1)))
    active = (padded > 0).astype(jnp.float32)
    sigma_x = conductivity(padded, sigma_table, 0)
    sigma_y = conductivity(padded, sigma_table, 1)
    sigma_z = conductivity(padded, sigma_table, 2)
    inner_x = harmonic(sigma_x[1:-1, :-1, 1:-1], sigma_x[1:-1, 1:, 1:-1])
    couple_x = inner_x * active[1:-1, :-1, 1:-1] * active[1:-1, 1:, 1:-1]
    inner_y = harmonic(sigma_y[1:-1, 1:-1, :-1], sigma_y[1:-1, 1:-1, 1:])
    couple_y = inner_y * active[1:-1, 1:-1, :-1] * active[1:-1, 1:-1, 1:]
    inner_z = harmonic(sigma_z[:-1, 1:-1, 1:-1], sigma_z[1:, 1:-1, 1:-1])
    couple_z = inner_z * active[:-1, 1:-1, 1:-1] * active[1:, 1:-1, 1:-1]
    centre_mask = active[1:-1, 1:-1, 1:-1]
    faces = (
        inner_x[:, :-1]
        + inner_x[:, 1:]
        + inner_y[:, :, :-1]
        + inner_y[:, :, 1:]
        + inner_z[:-1]
        + inner_z[1:]
    )
    diagonal = centre_mask * faces + (1.0 - centre_mask)
    return (centre_mask, diagonal, couple_x, couple_y, couple_z)


def operate(extended, terms):
    couple_x, couple_y, couple_z = (terms[2], terms[3], terms[4])
    centre = extended[:, 1:-1]
    widened = jnp.pad(centre, ((0, 0), (0, 0), (1, 1), (1, 1)))
    neighbours = (
        couple_x[:, :-1] * widened[:, :, :-2, 1:-1] + couple_x[:, 1:] * widened[:, :, 2:, 1:-1]
    )
    neighbours = (
        neighbours
        + couple_y[:, :, :-1] * widened[:, :, 1:-1, :-2]
        + couple_y[:, :, 1:] * widened[:, :, 1:-1, 2:]
    )
    neighbours = neighbours + couple_z[:-1] * extended[:, :-2] + couple_z[1:] * extended[:, 2:]
    return terms[1] * centre - neighbours


def smooth(extended, source, terms):
    image = operate(extended, terms)
    return extended[:, 1:-1] + OMEGA * terms[0] * (source - image) / terms[1]


def start(source, terms):
    return OMEGA * terms[0] * source / terms[1]


def leftover(extended, source, terms):
    return terms[0] * (source - operate(extended, terms))


def pair_matrix(length):
    rows_index = lax.broadcasted_iota(jnp.int32, (length, length // 2), 0)
    cols_index = lax.broadcasted_iota(jnp.int32, (length, length // 2), 1)
    return (rows_index // 2 == cols_index).astype(jnp.float32)


def pair_sum(values, along):
    if along == values.ndim - 1:
        return jnp.matmul(values, pair_matrix(values.shape[-1]), precision=lax.Precision.HIGHEST)
    folded = values.shape[:along] + (values.shape[along] // 2, 2) + values.shape[along + 1 :]
    return jnp.sum(values.reshape(folded), axis=along + 1)


def coarsen(terms):
    centre_mask, diagonal, couple_x, couple_y, couple_z = terms
    coarse_x = pair_sum(pair_sum(couple_x[:, 0::2], 0), 2)
    coarse_y = pair_sum(pair_sum(couple_y[:, :, 0::2], 0), 1)
    coarse_z = pair_sum(pair_sum(couple_z[0::2], 1), 2)
    internal = (
        pair_sum(pair_sum(couple_x[:, 1::2], 0), 2)
        + pair_sum(pair_sum(couple_y[:, :, 1::2], 0), 1)
        + pair_sum(pair_sum(couple_z[1::2], 1), 2)
    )
    counted = pair_sum(pair_sum(pair_sum(centre_mask, 0), 1), 2)
    raw_diag = pair_sum(pair_sum(pair_sum(centre_mask * diagonal, 0), 1), 2) - 2.0 * internal
    coarse_mask = jnp.minimum(counted, 1.0)
    coarse_diag = raw_diag + (1.0 - coarse_mask)
    return ((coarse_mask, coarse_diag, coarse_x, coarse_y, coarse_z), raw_diag)


def restrict(field):
    return pair_sum(pair_sum(pair_sum(field, 1), 2), 3)


def widen(field):
    sides, planes, rows_count, cols_count = field.shape
    spread = pair_matrix(2 * cols_count).T
    along_y = jnp.matmul(field, spread, precision=lax.Precision.HIGHEST)
    grown = jnp.broadcast_to(
        along_y[:, :, None, :, None, :], (sides, planes, 2, rows_count, 2, 2 * cols_count)
    )
    return grown.reshape(sides, 2 * planes, 2 * rows_count, 2 * cols_count)


def plane_total(values):
    return jnp.sum(values, axis=(-2, -1))


def line_terms(coarse_terms, raw_diag):
    line_diag = plane_total(raw_diag) - 2.0 * (
        plane_total(coarse_terms[2]) + plane_total(coarse_terms[3])
    )
    return (line_diag, plane_total(coarse_terms[4]))


def fine_rim(field):
    return extended_2(field, (("slab", 1),), 1)


def coarse_rim(field):
    return extended_2(field, (("slab", 1),), 1)


def on_device(rhs, labels, sigma_table):
    labels_near = extended_2(labels, (("slab", 0),), 1)
    own_terms = coefficients(labels_near, sigma_table)
    source = own_terms[0] * rhs
    fine_first = start(source, own_terms)
    fine_second = smooth(fine_rim(fine_first), source, own_terms)
    fine_left = leftover(fine_rim(fine_second), source, own_terms)
    coarse_terms, raw_diag = coarsen(own_terms)
    coarse_source = restrict(fine_left)
    coarse_first = start(coarse_source, coarse_terms)
    coarse_second = smooth(coarse_rim(coarse_first), coarse_source, coarse_terms)
    coarse_left = leftover(coarse_rim(coarse_second), coarse_source, coarse_terms)
    line_diag, line_faces = line_terms(coarse_terms, raw_diag)
    planes = line_diag.shape[0]
    local_rows = plane_total(coarse_left).T
    band = jnp.stack([line_diag, line_faces[:-1]], axis=1)
    all_rows, all_band = (
        lax.all_gather(local_rows, "slab", axis=0, tiled=True),
        lax.all_gather(band, "slab", axis=0, tiled=True),
    )
    lower_band = -all_band[:, 1]
    upper_band = -jnp.concatenate([all_band[1:, 1], jnp.zeros((1,), jnp.float32)])
    line_solution = lax.linalg.tridiagonal_solve(lower_band, all_band[:, 0], upper_band, all_rows)
    own_line = lax.dynamic_slice_in_dim(line_solution, lax.axis_index("slab") * planes, planes, 0)
    coarse_fix = coarse_second + coarse_terms[0] * own_line.T[:, :, None, None]
    coarse_post = smooth(coarse_rim(coarse_fix), coarse_source, coarse_terms)
    coarse_final = smooth(coarse_rim(coarse_post), coarse_source, coarse_terms)
    fine_third = fine_second + own_terms[0] * widen(coarse_final)
    fine_fourth = smooth(fine_rim(fine_third), source, own_terms)
    return smooth(fine_rim(fine_fourth), source, own_terms)


def solution(mesh):
    placed = (P("groups", "slab", None, None), P("slab", "groups", None), P())
    return jax.shard_map(
        on_device,
        mesh=mesh,
        in_specs=placed,
        out_specs=P("groups", "slab", None, None),
        check_vma=False,
    )
```

profile of v0, /device:TPU:8, one launch (start us, length us, event | category | flops | bytes accessed | tf_op | source)
XLA Modules:
  0.0 265.4 jit_solution(3007158552615316442)
XLA Ops:
  0.9 2.7 %collective-permute-start.1 = (s32[1,128,128]{2,1,0:T(8,128)S(1)}, s32[1,128,128]{2,1,0:T(8,128)S(1)}, u32[]{:S(2)}, u32[]{:S(2)}) collective-permute-start(s32[1,128,128]{2,1,0:T(8,128)S(1)} %get-tuple-element.28), channel_id=1, source_target_pairs={{1,0},{2,1},{3,2},{4,3},{5,4},{6,5},{7,6},{8,7},{9,8},{10,9},{11,1... | collective-permute-start | bytes 196616 | tf_op jit(solution)/shard_map/ppermute | solution.py:20
  3.7 1.9 collective-permute-start
  8.9 1.2 collective-permute-done
  10.5 11.2 %select_add_fusion.2 = (f32[6,130,130]{2,1,0:T(8,128)S(1)}, f32[6,130,130]{2,1,0:T(8,128)}, f32[6,130,130]{2,1,0:T(8,128)S(1)}) fusion(f32[]{:T(128)} %bitcast.6, f32[]{:T(128)} %bitcast.5, f32[]{:T(128)} %bitcast.4, f32[]{:T(128)} %bitcast.3, f32[]{:T(128)} %bitcast.2, s32[6,128,128]{2,1,0:T(8,128)S(1)} %pad_add_fusion, f32[]{:T(128)} %bitcast.16, ...), kind=kLoop, calls=%fused_computation.29 | loop fusion | flops 3244800 | bytes 1610076 | tf_op jit(solution)/shard_map/add | solution.py:32
  22.8 1.7 slice_multiply_fusion.2
  28.0 3.3 %collective-permute-start.3 = (f32[1,1,128,128]{3,2,1,0:T(8,128)}, f32[1,1,128,128]{3,2,1,0:T(8,128)}, u32[]{:S(2)}, u32[]{:S(2)}) collective-permute-start(f32[1,1,128,128]{3,2,1,0:T(8,128)} %get-tuple-element.26), channel_id=1, source_target_pairs={{1,0},{2,1},{3,2},{4,3},{5,4},{6,5},{7,6},{8,7},{9,8},{10,9},{11,1... | collective-permute-start | bytes 196616 | tf_op jit(solution)/shard_map/ppermute | solution.py:20
  31.3 1.9 collective-permute-start.2
  33.2 4.6 %slice.1109 = f32[4,128,64]{2,1,0:T(8,128)S(1)} slice(f32[4,128,129]{2,1,0:T(8,128)S(1)} %get-tuple-element.10), slice={[0:4:1], [0:128:1], [1:129:2]} | slice | bytes 262144 | tf_op jit(solution)/shard_map/slice | solution.py:110
  45.9 4.5 %slice.1116 = f32[4,128,65]{2,1,0:T(8,128)S(1)} slice(f32[4,128,129]{2,1,0:T(8,128)S(1)} %get-tuple-element.10), slice={[0:4:1], [0:128:1], [0:129:2]} | slice | bytes 266240 | tf_op jit(solution)/shard_map/slice | solution.py:106
  52.2 1.2 fusion.13
  54.1 4.5 %collective-permute-start.5 = (f32[1,1,128,128]{3,2,1,0:T(8,128)}, f32[1,1,128,128]{3,2,1,0:T(8,128)S(1)}, u32[]{:S(2)}, u32[]{:S(2)}) collective-permute-start(f32[1,1,128,128]{3,2,1,0:T(8,128)} %get-tuple-element.24), channel_id=1, source_target_pairs={{1,0},{2,1},{3,2},{4,3},{5,4},{6,5},{7,6},{8,7},{9,8},{10,9},{11,1... | collective-permute-start | bytes 196616 | tf_op jit(solution)/shard_map/ppermute | solution.py:20
  58.6 1.9 collective-permute-start.4
  60.9 4.4 %collective-permute-done.4 = f32[1,1,128,128]{3,2,1,0:T(8,128)S(1)} collective-permute-done((f32[1,1,128,128]{3,2,1,0:T(8,128)}, f32[1,1,128,128]{3,2,1,0:T(8,128)S(1)}, u32[]{:S(2)}, u32[]{:S(2)}) %collective-permute-start.4) | collective-permute-done | bytes 65568 | tf_op jit(solution)/shard_map/ppermute | solution.py:19
  66.9 15.3 %all-gather.1 = f32[16,2,2]{2,1,0:T(2,128)S(1)} all-gather(f32[1,2,2]{2,1,0:T(2,128)S(1)} %bitcast.570), channel_id=1, replica_groups=mesh['groups'=2,'slab'=16] {'slab'}, dimensions={0}, use_global_device_ids=true | all-gather | bytes 272 | tf_op jit(solution)/shard_map/all_gather | solution.py:171
  83.7 6.0 %collective-permute-start.7 = (f32[1,1,64,64]{3,2,1,0:T(8,128)S(1)}, f32[1,1,64,64]{3,2,1,0:T(8,128)S(1)}, u32[]{:S(2)}, u32[]{:S(2)}) collective-permute-start(f32[1,1,64,64]{3,2,1,0:T(8,128)S(1)} %get-tuple-element.40), channel_id=1, source_target_pairs={{1,0},{2,1},{3,2},{4,3},{5,4},{6,5},{7,6},{8,7},{9,8},{10,9},{11,1... | collective-permute-start | bytes 49160 | tf_op jit(solution)/shard_map/ppermute | solution.py:20
  89.7 1.9 collective-permute-start.6
  94.0 1.8 collective-permute-done.6
  96.0 2.8 %collective-permute-start.9 = (f32[1,1,64,64]{3,2,1,0:T(8,128)S(1)}, f32[1,1,64,64]{3,2,1,0:T(8,128)S(1)}, u32[]{:S(2)}, u32[]{:S(2)}) collective-permute-start(f32[1,1,64,64]{3,2,1,0:T(8,128)S(1)} %get-tuple-element.36), channel_id=1, source_target_pairs={{1,0},{2,1},{3,2},{4,3},{5,4},{6,5},{7,6},{8,7},{9,8},{10,9},{11,1... | collective-permute-start | bytes 49160 | tf_op jit(solution)/shard_map/ppermute | solution.py:20
  98.7 2.1 collective-permute-start.8
  160.8 24.9 %all-reduce.9 = f32[32]{0:T(128)S(1)} all-reduce(f32[32]{0:T(128)S(1)} %dynamic-update-slice), channel_id=2, replica_groups=mesh['groups'=2,'slab'=16] {'slab'}, use_global_device_ids=true, to_apply=%add.9 | all-reduce | flops 32 | bytes 256
  228.9 1.9 collective-permute-start.11
  230.8 2.4 collective-permute-start.10
  233.2 3.7 %collective-permute-done.10 = f32[1,1,64,64]{3,2,1,0:T(8,128)S(1)} collective-permute-done((f32[1,1,64,64]{3,2,1,0:T(8,128)S(1)}, f32[1,1,64,64]{3,2,1,0:T(8,128)S(1)}, u32[]{:S(2)}, u32[]{:S(2)}) %collective-permute-start.10) | collective-permute-done | bytes 16416 | tf_op jit(solution)/shard_map/ppermute | solution.py:19
  237.1 2.7 %collective-permute-start.13 = (f32[1,1,64,64]{3,2,1,0:T(8,128)S(1)}, f32[1,1,64,64]{3,2,1,0:T(8,128)S(1)}, u32[]{:S(2)}, u32[]{:S(2)}) collective-permute-start(f32[1,1,64,64]{3,2,1,0:T(8,128)S(1)} %get-tuple-element.30), channel_id=1, source_target_pairs={{1,0},{2,1},{3,2},{4,3},{5,4},{6,5},{7,6},{8,7},{9,8},{10,9},{11,1... | collective-permute-start | bytes 49160 | tf_op jit(solution)/shard_map/ppermute | solution.py:20
  239.8 1.9 collective-permute-start.12
  241.7 4.8 %collective-permute-done.12 = f32[1,1,64,64]{3,2,1,0:T(8,128)S(1)} collective-permute-done((f32[1,1,64,64]{3,2,1,0:T(8,128)S(1)}, f32[1,1,64,64]{3,2,1,0:T(8,128)S(1)}, u32[]{:S(2)}, u32[]{:S(2)}) %collective-permute-start.12) | collective-permute-done | bytes 16416 | tf_op jit(solution)/shard_map/ppermute | solution.py:19
  247.1 1.9 collective-permute-start.15
  249.0 2.4 collective-permute-start.14
  251.4 4.1 %collective-permute-done.14 = f32[1,1,128,128]{3,2,1,0:T(8,128)S(1)} collective-permute-done((f32[1,1,128,128]{3,2,1,0:T(8,128)S(1)}, f32[1,1,128,128]{3,2,1,0:T(8,128)S(1)}, u32[]{:S(2)}, u32[]{:S(2)}) %collective-permute-start.14) | collective-permute-done | bytes 65568 | tf_op jit(solution)/shard_map/ppermute | solution.py:19
  255.9 1.9 collective-permute-start.17
  257.9 2.4 collective-permute-start.16
  260.3 4.1 %collective-permute-done.16 = f32[1,1,128,128]{3,2,1,0:T(8,128)S(1)} collective-permute-done((f32[1,1,128,128]{3,2,1,0:T(8,128)S(1)}, f32[1,1,128,128]{3,2,1,0:T(8,128)S(1)}, u32[]{:S(2)}, u32[]{:S(2)}) %collective-permute-start.16) | collective-permute-done | bytes 65568 | tf_op jit(solution)/shard_map/ppermute | solution.py:19
  (124 shorter events, 29.7 us)
Async XLA Ops:
  0.0 10.1 %copy-start.4 = (s32[4,128,128]{2,1,0:T(8,128)S(1)}, s32[4,128,128]{2,1,0:T(8,128)}, u32[]{:S(2)}) copy-start(s32[4,128,128]{2,1,0:T(8,128)} %param.4) | copy-start | bytes 786436
  0.9 8.0 %collective-permute-start.1 = (s32[1,128,128]{2,1,0:T(8,128)S(1)}, s32[1,128,128]{2,1,0:T(8,128)S(1)}, u32[]{:S(2)}, u32[]{:S(2)}) collective-permute-start(s32[1,128,128]{2,1,0:T(8,128)S(1)} %get-tuple-element.28), channel_id=1, source_target_pairs={{1,0},{2,1},{3,2},{4,3},{5,4},{6,5},{7,6},{8,7},{9,8},{10,9},{11,1... | collective-permute-start | bytes 196616 | tf_op jit(solution)/shard_map/ppermute | solution.py:20
  3.7 6.5 %collective-permute-start = (s32[1,128,128]{2,1,0:T(8,128)S(1)}, s32[1,128,128]{2,1,0:T(8,128)S(1)}, u32[]{:S(2)}, u32[]{:S(2)}) collective-permute-start(s32[1,128,128]{2,1,0:T(8,128)S(1)} %get-tuple-element.27), channel_id=1, source_target_pairs={{0,1},{1,2},{2,3},{3,4},{4,5},{5,6},{6,7},{7,8},{8,9},{9,10},{10,1... | collective-permute-start | bytes 196616 | tf_op jit(solution)/shard_map/ppermute | solution.py:19
  26.2 1.0 copy-start.9
  28.0 24.2 %collective-permute-start.3 = (f32[1,1,128,128]{3,2,1,0:T(8,128)}, f32[1,1,128,128]{3,2,1,0:T(8,128)}, u32[]{:S(2)}, u32[]{:S(2)}) collective-permute-start(f32[1,1,128,128]{3,2,1,0:T(8,128)} %get-tuple-element.26), channel_id=1, source_target_pairs={{1,0},{2,1},{3,2},{4,3},{5,4},{6,5},{7,6},{8,7},{9,8},{10,9},{11,1... | collective-permute-start | bytes 196616 | tf_op jit(solution)/shard_map/ppermute | solution.py:20
  31.3 20.9 %collective-permute-start.2 = (f32[1,1,128,128]{3,2,1,0:T(8,128)}, f32[1,1,128,128]{3,2,1,0:T(8,128)}, u32[]{:S(2)}, u32[]{:S(2)}) collective-permute-start(f32[1,1,128,128]{3,2,1,0:T(8,128)} %get-tuple-element.25), channel_id=1, source_target_pairs={{0,1},{1,2},{2,3},{3,4},{4,5},{5,6},{6,7},{7,8},{8,9},{9,10},{10,1... | collective-permute-start | bytes 196616 | tf_op jit(solution)/shard_map/ppermute | solution.py:19
  37.8 0.9 copy-start.6
  38.8 0.9 copy-start.7
  39.8 0.9 copy-start.8
  39.8 1.7 copy-start.5
  42.6 1.1 copy-start.3
  44.2 0.8 copy-start.10
  44.2 0.9 copy-start.11
  45.9 4.6 %copy-start.13 = (f32[2,64,64]{1,2,0:T(8,128)S(1)}, f32[2,64,64]{1,2,0:T(8,128)}, u32[]{:S(2)}) copy-start(f32[2,64,64]{1,2,0:T(8,128)} %get-tuple-element.38) | copy-start | bytes 98308
  50.5 0.8 copy-start.12
  54.1 6.9 %collective-permute-start.5 = (f32[1,1,128,128]{3,2,1,0:T(8,128)}, f32[1,1,128,128]{3,2,1,0:T(8,128)S(1)}, u32[]{:S(2)}, u32[]{:S(2)}) collective-permute-start(f32[1,1,128,128]{3,2,1,0:T(8,128)} %get-tuple-element.24), channel_id=1, source_target_pairs={{1,0},{2,1},{3,2},{4,3},{5,4},{6,5},{7,6},{8,7},{9,8},{10,9},{11,1... | collective-permute-start | bytes 196616 | tf_op jit(solution)/shard_map/ppermute | solution.py:20
  58.6 6.7 %collective-permute-start.4 = (f32[1,1,128,128]{3,2,1,0:T(8,128)}, f32[1,1,128,128]{3,2,1,0:T(8,128)S(1)}, u32[]{:S(2)}, u32[]{:S(2)}) collective-permute-start(f32[1,1,128,128]{3,2,1,0:T(8,128)} %get-tuple-element.23), channel_id=1, source_target_pairs={{0,1},{1,2},{2,3},{3,4},{4,5},{5,6},{6,7},{7,8},{8,9},{9,10},{10,1... | collective-permute-start | bytes 196616 | tf_op jit(solution)/shard_map/ppermute | solution.py:19
  65.8 0.8 copy-start
  83.6 12.2 %copy-start.2 = (f32[2,64,64]{2,1,0:T(8,128)S(1)}, f32[2,64,64]{2,1,0:T(8,128)}, u32[]{:S(2)}) copy-start(f32[2,64,64]{2,1,0:T(8,128)} %copy.35) | copy-start | bytes 98308
  83.7 12.2 %copy-start.1 = (f32[2,64,64]{2,1,0:T(8,128)S(1)}, f32[2,64,64]{2,1,0:T(8,128)}, u32[]{:S(2)}) copy-start(f32[2,64,64]{2,1,0:T(8,128)} %copy.36) | copy-start | bytes 98308
  83.7 10.4 %collective-permute-start.7 = (f32[1,1,64,64]{3,2,1,0:T(8,128)S(1)}, f32[1,1,64,64]{3,2,1,0:T(8,128)S(1)}, u32[]{:S(2)}, u32[]{:S(2)}) collective-permute-start(f32[1,1,64,64]{3,2,1,0:T(8,128)S(1)} %get-tuple-element.40), channel_id=1, source_target_pairs={{1,0},{2,1},{3,2},{4,3},{5,4},{6,5},{7,6},{8,7},{9,8},{10,9},{11,1... | collective-permute-start | bytes 49160 | tf_op jit(solution)/shard_map/ppermute | solution.py:20
  89.7 6.1 %collective-permute-start.6 = (f32[1,1,64,64]{3,2,1,0:T(8,128)S(1)}, f32[1,1,64,64]{3,2,1,0:T(8,128)S(1)}, u32[]{:S(2)}, u32[]{:S(2)}) collective-permute-start(f32[1,1,64,64]{3,2,1,0:T(8,128)S(1)} %get-tuple-element.39), channel_id=1, source_target_pairs={{0,1},{1,2},{2,3},{3,4},{4,5},{5,6},{6,7},{7,8},{8,9},{9,10},{10,1... | collective-permute-start | bytes 49160 | tf_op jit(solution)/shard_map/ppermute | solution.py:19
  96.0 64.4 %collective-permute-start.9 = (f32[1,1,64,64]{3,2,1,0:T(8,128)S(1)}, f32[1,1,64,64]{3,2,1,0:T(8,128)S(1)}, u32[]{:S(2)}, u32[]{:S(2)}) collective-permute-start(f32[1,1,64,64]{3,2,1,0:T(8,128)S(1)} %get-tuple-element.36), channel_id=1, source_target_pairs={{1,0},{2,1},{3,2},{4,3},{5,4},{6,5},{7,6},{8,7},{9,8},{10,9},{11,1... | collective-permute-start | bytes 49160 | tf_op jit(solution)/shard_map/ppermute | solution.py:20
  98.7 61.6 %collective-permute-start.8 = (f32[1,1,64,64]{3,2,1,0:T(8,128)S(1)}, f32[1,1,64,64]{3,2,1,0:T(8,128)S(1)}, u32[]{:S(2)}, u32[]{:S(2)}) collective-permute-start(f32[1,1,64,64]{3,2,1,0:T(8,128)S(1)} %get-tuple-element.35), channel_id=1, source_target_pairs={{0,1},{1,2},{2,3},{3,4},{4,5},{5,6},{6,7},{7,8},{8,9},{9,10},{10,1... | collective-permute-start | bytes 49160 | tf_op jit(solution)/shard_map/ppermute | solution.py:19
  228.9 4.3 %collective-permute-start.11 = (f32[1,1,64,64]{3,2,1,0:T(8,128)S(1)}, f32[1,1,64,64]{3,2,1,0:T(8,128)S(1)}, u32[]{:S(2)}, u32[]{:S(2)}) collective-permute-start(f32[1,1,64,64]{3,2,1,0:T(8,128)S(1)} %get-tuple-element.32), channel_id=1, source_target_pairs={{1,0},{2,1},{3,2},{4,3},{5,4},{6,5},{7,6},{8,7},{9,8},{10,9},{11,1... | collective-permute-start | bytes 49160 | tf_op jit(solution)/shard_map/ppermute | solution.py:20
  230.8 6.1 %collective-permute-start.10 = (f32[1,1,64,64]{3,2,1,0:T(8,128)S(1)}, f32[1,1,64,64]{3,2,1,0:T(8,128)S(1)}, u32[]{:S(2)}, u32[]{:S(2)}) collective-permute-start(f32[1,1,64,64]{3,2,1,0:T(8,128)S(1)} %get-tuple-element.31), channel_id=1, source_target_pairs={{0,1},{1,2},{2,3},{3,4},{4,5},{5,6},{6,7},{7,8},{8,9},{9,10},{10,1... | collective-permute-start | bytes 49160 | tf_op jit(solution)/shard_map/ppermute | solution.py:19
  237.1 4.6 %collective-permute-start.13 = (f32[1,1,64,64]{3,2,1,0:T(8,128)S(1)}, f32[1,1,64,64]{3,2,1,0:T(8,128)S(1)}, u32[]{:S(2)}, u32[]{:S(2)}) collective-permute-start(f32[1,1,64,64]{3,2,1,0:T(8,128)S(1)} %get-tuple-element.30), channel_id=1, source_target_pairs={{1,0},{2,1},{3,2},{4,3},{5,4},{6,5},{7,6},{8,7},{9,8},{10,9},{11,1... | collective-permute-start | bytes 49160 | tf_op jit(solution)/shard_map/ppermute | solution.py:20
  239.8 6.8 %collective-permute-start.12 = (f32[1,1,64,64]{3,2,1,0:T(8,128)S(1)}, f32[1,1,64,64]{3,2,1,0:T(8,128)S(1)}, u32[]{:S(2)}, u32[]{:S(2)}) collective-permute-start(f32[1,1,64,64]{3,2,1,0:T(8,128)S(1)} %get-tuple-element.29), channel_id=1, source_target_pairs={{0,1},{1,2},{2,3},{3,4},{4,5},{5,6},{6,7},{7,8},{8,9},{9,10},{10,1... | collective-permute-start | bytes 49160 | tf_op jit(solution)/shard_map/ppermute | solution.py:19
  247.1 4.3 %collective-permute-start.15 = (f32[1,1,128,128]{3,2,1,0:T(8,128)S(1)}, f32[1,1,128,128]{3,2,1,0:T(8,128)S(1)}, u32[]{:S(2)}, u32[]{:S(2)}) collective-permute-start(f32[1,1,128,128]{3,2,1,0:T(8,128)S(1)} %get-tuple-element.22), channel_id=1, source_target_pairs={{1,0},{2,1},{3,2},{4,3},{5,4},{6,5},{7,6},{8,7},{9,8},{10,9},{11,1... | collective-permute-start | bytes 196616 | tf_op jit(solution)/shard_map/ppermute | solution.py:20
  249.0 6.5 %collective-permute-start.14 = (f32[1,1,128,128]{3,2,1,0:T(8,128)S(1)}, f32[1,1,128,128]{3,2,1,0:T(8,128)S(1)}, u32[]{:S(2)}, u32[]{:S(2)}) collective-permute-start(f32[1,1,128,128]{3,2,1,0:T(8,128)S(1)} %get-tuple-element.21), channel_id=1, source_target_pairs={{0,1},{1,2},{2,3},{3,4},{4,5},{5,6},{6,7},{7,8},{8,9},{9,10},{10,1... | collective-permute-start | bytes 196616 | tf_op jit(solution)/shard_map/ppermute | solution.py:19
  255.9 4.3 %collective-permute-start.17 = (f32[1,1,128,128]{3,2,1,0:T(8,128)S(1)}, f32[1,1,128,128]{3,2,1,0:T(8,128)S(1)}, u32[]{:S(2)}, u32[]{:S(2)}) collective-permute-start(f32[1,1,128,128]{3,2,1,0:T(8,128)S(1)} %get-tuple-element.20), channel_id=1, source_target_pairs={{1,0},{2,1},{3,2},{4,3},{5,4},{6,5},{7,6},{8,7},{9,8},{10,9},{11,1... | collective-permute-start | bytes 196616 | tf_op jit(solution)/shard_map/ppermute | solution.py:20
  257.9 6.5 %collective-permute-start.16 = (f32[1,1,128,128]{3,2,1,0:T(8,128)S(1)}, f32[1,1,128,128]{3,2,1,0:T(8,128)S(1)}, u32[]{:S(2)}, u32[]{:S(2)}) collective-permute-start(f32[1,1,128,128]{3,2,1,0:T(8,128)S(1)} %get-tuple-element.19), channel_id=1, source_target_pairs={{0,1},{1,2},{2,3},{3,4},{4,5},{5,6},{6,7},{7,8},{8,9},{9,10},{10,1... | collective-permute-start | bytes 196616 | tf_op jit(solution)/shard_map/ppermute | solution.py:19
  (2 other events, 1.3 us)
where the time goes:
time: 268 us; the launch traced here: 265 us
  between operations  101 us (38%)
  starting transfers between devices  46.7 us (17%)
  blocking collectives  40.2 us (15%)
  local copies, waits for them, and re-layouts  28.7 us (11%)
  waiting for transfers between devices  24.1 us (9%)
  other arithmetic  21.2 us (8%)
  matrix products  3.07 us (1%)
    ppermute x9, starting transfers between devices, extended_2(): after = lax.ppermute(first, axis, down)  27.8 us
    unnamed x1, blocking collectives  24.9 us
    ppermute x9, waiting for transfers between devices, extended_2(): before = lax.ppermute(last, axis, up)  24.1 us
    ppermute x9, starting transfers between devices, extended_2(): before = lax.ppermute(last, axis, up)  18.9 us
    all_gather x1, blocking collectives, on_device(): lax.all_gather(band, 'slab', axis=0, tiled=True)  15.3 us
    add x1, other arithmetic, conductivity(): running + jnp.where(padded == tissue, sigma_table[tissue, column], 0.0)  11.2 us
    unnamed x39, local copies, waits for them, and re-layouts  7.66 us
    slice x8, local copies, waits for them, and re-layouts, on_device(): lax.linalg.tridiagonal_solve(lower_band, all_band[:, 0], upper_band, all_...  5.56 us
  transfers between devices with their start and end apart: 18, of which 7 were waited for; matrix products, arithmetic and copies ran while one was open for 8% of the time, Pallas kernels for 0%

commit v1 on v0

v1 whole, which is shorter than its diff:
```python
import functools

import jax
import jax.numpy as jnp
from jax import lax
from jax.experimental import pallas as pl
from jax.experimental.pallas import tpu as pltpu
from jax.sharding import PartitionSpec as P

OMEGA = 0.8
LABELS = 5
MESH = pl.DeviceIdType.MESH


def copy_to(src, dst, sems, slot, target):
    return pltpu.make_async_remote_copy(
        src_ref=src,
        dst_ref=dst,
        send_sem=sems.at[0, slot],
        recv_sem=sems.at[1, slot],
        device_id={"slab": target},
        device_id_type=MESH,
    )


def kernel(
    n, rhs_hbm, lab_hbm, table, out_hbm,
    lab, rhs, gx, gxr, gy, gyr, gzl, gzh, idf, dg, ua, ub, tmp, pro,
    cof, d1, b1, vn, far_out, far_in, line_out, line_all, row_out, row_all, xs, outv,
    load_sem, sems, gather_sem,
):
    me = lax.axis_index("slab")
    nx, ny = lab.shape[1:]
    hx_rows = nx // 2
    has_low, has_up = me > 0, me < n - 1
    has_low2, has_up2 = me > 1, me < n - 2

    own_lab = pltpu.make_async_copy(lab_hbm, lab.at[pl.ds(3, 4)], load_sem.at[0])
    own_rhs = pltpu.make_async_copy(rhs_hbm.at[0], rhs.at[pl.ds(2, 4)], load_sem.at[1])
    own_lab.start()
    own_rhs.start()

    barrier = pltpu.get_barrier_semaphore()

    def greet(step, carry):
        other = lax.rem(me + step, n)
        pl.semaphore_signal(barrier, inc=1, device_id={"slab": other}, device_id_type=MESH)
        return carry

    lax.fori_loop(1, n, greet, 0)
    pl.semaphore_wait(barrier, n - 1)

    up, low = lax.rem(me + 1, n), lax.rem(me + n - 1, n)
    up2, low2 = lax.rem(me + 2, n), lax.rem(me + n - 2, n)

    lab_up = copy_to(lab_hbm.at[pl.ds(1, 3)], lab.at[pl.ds(0, 3)], sems, 0, up)
    lab_low = copy_to(lab_hbm.at[pl.ds(0, 3)], lab.at[pl.ds(7, 3)], sems, 1, low)
    rhs_up = copy_to(rhs_hbm.at[0, pl.ds(2, 2)], rhs.at[pl.ds(0, 2)], sems, 2, up)
    rhs_low = copy_to(rhs_hbm.at[0, pl.ds(0, 2)], rhs.at[pl.ds(6, 2)], sems, 3, low)
    cof_up = copy_to(cof.at[1], cof.at[0], sems, 4, up)
    cof_low = copy_to(cof.at[1], cof.at[2], sems, 5, low)
    b1_up = copy_to(b1.at[1], b1.at[0], sems, 6, up)
    b1_low = copy_to(b1.at[1], b1.at[2], sems, 7, low)
    u2_up = copy_to(ub.at[4], ub.at[0], sems, 8, up)
    u2_low = copy_to(ub.at[3], ub.at[7], sems, 9, low)
    vn_up = copy_to(vn.at[1], vn.at[0], sems, 10, up)
    vn_low = copy_to(vn.at[1], vn.at[2], sems, 11, low)
    far_up = copy_to(far_out.at[0], far_in.at[0], sems, 12, up2)
    far_low = copy_to(far_out.at[1], far_in.at[1], sems, 13, low2)

    def send(upward, downward):
        pl.when(has_up)(upward.start)
        pl.when(has_low)(downward.start)

    def receive(upward, downward):
        pl.when(has_low)(upward.wait_recv)
        pl.when(has_up)(downward.wait_recv)

    send(lab_up, lab_low)
    send(rhs_up, rhs_low)

    def clear(ref, first, count):
        for k in range(first, first + count):
            ref[k] = jnp.zeros(ref.shape[1:], ref.dtype)

    @pl.when(me == 0)
    def _():
        clear(lab, 0, 3)
        clear(rhs, 0, 2)
        clear(cof.at[0], 0, 5)
        clear(b1, 0, 1)
        clear(ub, 0, 1)
        clear(vn, 0, 1)

    @pl.when(me == n - 1)
    def _():
        clear(lab, 7, 3)
        clear(rhs, 6, 2)
        clear(cof.at[2], 0, 5)
        clear(b1, 2, 1)
        clear(ub, 7, 1)
        clear(vn, 2, 1)

    @pl.when(me < 2)
    def _():
        clear(far_in, 0, 1)

    @pl.when(me >= n - 2)
    def _():
        clear(far_in, 1, 1)

    xs[...] = jnp.zeros(xs.shape, xs.dtype)

    fine_row = lax.broadcasted_iota(jnp.int32, (nx, ny), 0) % 2 == 1
    fine_lane = lax.broadcasted_iota(jnp.int32, (nx, ny), 1) % 2 == 1
    even = lax.broadcasted_iota(jnp.int32, (hx_rows, ny), 1) % 2 == 0

    def select(values, column):
        chosen = jnp.full(values.shape, table[0, column], jnp.float32)
        for tissue in range(1, LABELS):
            chosen = jnp.where(values == tissue, table[tissue, column], chosen)
        return chosen

    def harmonic(a, b):
        return 2.0 * a * b / (a + b)

    def plane_terms(k):
        here, below, above = lab[k + 1], lab[k], lab[k + 2]
        a = (here > 0).astype(jnp.float32)
        sx, sy, sz = select(here, 0), select(here, 1), select(here, 2)
        hx = harmonic(pltpu.roll(sx, 1, 0), sx)
        faces = hx + pltpu.roll(hx, nx - 1, 0)
        cx = hx * a * pltpu.roll(a, 1, 0)
        gx[k] = cx
        gxr[k] = pltpu.roll(cx, nx - 1, 0)
        hy = harmonic(pltpu.roll(sy, 1, 1), sy)
        faces = faces + hy + pltpu.roll(hy, ny - 1, 1)
        cy = hy * a * pltpu.roll(a, 1, 1)
        gy[k] = cy
        gyr[k] = pltpu.roll(cy, ny - 1, 1)
        hl = harmonic(select(below, 2), sz)
        gzl[k] = hl * a * (below > 0).astype(jnp.float32)
        hh = harmonic(sz, select(above, 2))
        gzh[k] = hh * a * (above > 0).astype(jnp.float32)
        faces = faces + hl + hh
        diagonal = a * faces + (1.0 - a)
        dg[k] = diagonal
        idf[k] = OMEGA * a / diagonal

    def over(first, last, body):
        def step(k, carry):
            body(k)
            return carry

        lax.fori_loop(first, last, step, 0)

    own_lab.wait()
    receive(lab_up, lab_low)
    over(0, 8, plane_terms)

    def rows_even(plane):
        tmp[0] = plane
        return tmp[0, pl.ds(0, hx_rows, 2), :]

    def rows_sum(plane):
        tmp[0] = plane
        return tmp[0, pl.ds(0, hx_rows, 2), :] + tmp[0, pl.ds(1, hx_rows, 2), :]

    def lanes_sum(t0, t1):
        return jnp.where(even, t0 + pltpu.roll(t0, ny - 1, 1), t1 + pltpu.roll(t1, 1, 1))

    def lanes_even(t0, t1):
        return jnp.where(even, t0, pltpu.roll(t1, 1, 1))

    def restrict(p0, p1):
        return lanes_sum(rows_sum(p0), rows_sum(p1))

    def inner(k):
        mask = (idf[k] > 0.0).astype(jnp.float32)
        doubled = jnp.where(fine_row, gx[k], 0.0) + jnp.where(fine_lane, gy[k], 0.0)
        if k % 2 == 1:
            doubled = doubled + gzl[k]
        return mask * dg[k] - 2.0 * doubled, mask

    (f0, m0), (f1, m1), (f2, m2), (f3, m3) = inner(2), inner(3), inner(4), inner(5)
    raw = restrict(f0 + f1, f2 + f3)
    active1 = jnp.minimum(restrict(m0 + m1, m2 + m3), 1.0)
    diag1 = raw + (1.0 - active1)
    d1[...] = diag1
    cof[1, 0] = OMEGA * active1 / diag1
    coarse_x = lanes_sum(rows_even(gx[2] + gx[3]), rows_even(gx[4] + gx[5]))
    coarse_y = lanes_even(rows_sum(gy[2] + gy[3]), rows_sum(gy[4] + gy[5]))
    coarse_zl = restrict(gzl[2], gzl[4])
    cof[1, 1] = coarse_x
    cof[1, 2] = coarse_y
    cof[1, 3] = coarse_zl
    cof[1, 4] = restrict(gzh[3], gzh[5])
    send(cof_up, cof_low)

    def plane_sums(packed):
        lower = jnp.sum(jnp.where(even, packed, 0.0), axis=0, keepdims=True)
        upper = jnp.sum(jnp.where(even, 0.0, packed), axis=0, keepdims=True)
        lower = jnp.sum(lower, axis=1, keepdims=True)
        upper = jnp.sum(upper, axis=1, keepdims=True)
        return lower, upper

    sub = lax.broadcasted_iota(jnp.int32, (8, ny), 0)

    def gather(out, everyone, slot, values):
        tile = jnp.zeros((8, ny), jnp.float32)
        for row, value in enumerate(values):
            tile = jnp.where(sub == row, value, tile)
        out[...] = tile
        everyone[me] = tile

        def one(step, carry):
            pltpu.make_async_remote_copy(
                src_ref=out,
                dst_ref=everyone.at[me],
                send_sem=gather_sem.at[0, slot],
                recv_sem=gather_sem.at[1, slot],
                device_id={"slab": lax.rem(me + step, n)},
                device_id_type=MESH,
            ).start()
            return carry

        lax.fori_loop(1, n, one, 0)

    def gather_wait(everyone, side, slot):
        rest = everyone.at[pl.ds(0, n - 1)]
        pltpu.make_async_copy(rest, rest, gather_sem.at[side, slot]).wait()

    dl, du = plane_sums(raw - 2.0 * (coarse_x + coarse_y))
    fl, fu = plane_sums(coarse_zl)
    gather(line_out, line_all, 0, (dl, du, fl, fu))

    own_rhs.wait()
    receive(rhs_up, rhs_low)

    def first_sweep(k):
        ua[k] = idf[k] * rhs[k]

    over(0, 8, first_sweep)

    def neighbours(field, k):
        u = field[k]
        total = gx[k] * pltpu.roll(u, 1, 0) + gxr[k] * pltpu.roll(u, nx - 1, 0)
        total = total + gy[k] * pltpu.roll(u, 1, 1) + gyr[k] * pltpu.roll(u, ny - 1, 1)
        return u, total + gzl[k] * field[k - 1] + gzh[k] * field[k + 1]

    def sweep(src, dst, shift=0):
        def body(k):
            u, total = neighbours(src, k)
            dst[k - shift] = (1.0 - OMEGA) * u + idf[k] * (rhs[k] + total)

        return body

    over(1, 7, sweep(ua, ub))

    def residual(k):
        u, total = neighbours(ub, k)
        return jnp.where(idf[k] > 0.0, rhs[k] - dg[k] * u + total, 0.0)

    b1[1] = restrict(residual(2) + residual(3), residual(4) + residual(5))
    send(b1_up, b1_low)

    gather_wait(line_all, 1, 0)
    flat = line_all.reshape(n * 8, ny)

    def line_rows(ref, row):
        return ref[pl.ds(row, n, 8), :]

    de, do, fe, fo = (line_rows(flat, row) for row in range(4))

    def back(x, s):
        return pltpu.roll(x, s % n, 0)

    def ahead(x, s):
        return pltpu.roll(x, (n - s) % n, 0)

    inv_odd = 1.0 / do
    to_low = fe * back(inv_odd, 1)
    to_up = fo * inv_odd
    fe_next = ahead(fe, 1)
    diag = de - fe * to_low - fo * to_up
    lower = -to_low * back(fo, 1)
    upper = -to_up * fe_next
    steps = []
    shift = 1
    while shift < n:
        alpha, gamma = lower / back(diag, shift), upper / ahead(diag, shift)
        steps.append((shift, alpha, gamma))
        diag = diag - alpha * back(upper, shift) - gamma * ahead(lower, shift)
        lower, upper = -alpha * back(lower, shift), -gamma * ahead(upper, shift)
        shift *= 2
    inv_diag = 1.0 / diag

    receive(cof_up, cof_low)
    receive(b1_up, b1_low)
    send(u2_up, u2_low)

    zero = jnp.zeros((hx_rows, ny), jnp.float32)

    def coarse_neighbours(k, below, f, above):
        cx, cy = cof[k, 1], cof[k, 2]
        zl = jnp.where(even, pltpu.roll(below, ny - 1, 1), pltpu.roll(f, 1, 1))
        zh = jnp.where(even, pltpu.roll(f, ny - 1, 1), pltpu.roll(above, 1, 1))
        total = cx * pltpu.roll(f, 1, 0)
        total = total + pltpu.roll(cx, hx_rows - 1, 0) * pltpu.roll(f, hx_rows - 1, 0)
        total = total + cy * pltpu.roll(f, 2, 1)
        total = total + pltpu.roll(cy, ny - 2, 1) * pltpu.roll(f, ny - 2, 1)
        return total + cof[k, 3] * zl + cof[k, 4] * zh

    def coarse_sweep(fields):
        swept = []
        for k in range(3):
            total = coarse_neighbours(k, fields[k], fields[k + 1], fields[k + 2])
            swept.append((1.0 - OMEGA) * fields[k + 1] + cof[k, 0] * (b1[k] + total))
        return [zero] + swept + [zero]

    v1 = [zero] + [cof[k, 0] * b1[k] for k in range(3)] + [zero]
    v2 = coarse_sweep(v1)
    own_total = coarse_neighbours(1, v2[1], v2[2], v2[3])
    r1 = jnp.where(cof[1, 0] > 0.0, b1[1] - d1[...] * v2[2] + own_total, 0.0)
    gather(row_out, row_all, 1, plane_sums(r1))
    vn[1] = v2[2]
    far_out[0] = jnp.where(even, pltpu.roll(cof[1, 0], ny - 1, 1), v2[2])
    far_out[1] = jnp.where(even, v2[2], pltpu.roll(cof[1, 0], 1, 1))
    send(vn_up, vn_low)
    pl.when(has_up2)(far_up.start)
    pl.when(has_low2)(far_low.start)

    gather_wait(row_all, 1, 1)
    flat_rows = row_all.reshape(n * 8, ny)
    be, bo = line_rows(flat_rows, 0), line_rows(flat_rows, 1)
    reduced = be + to_low * back(bo, 1) + to_up * bo
    for shift, alpha, gamma in steps:
        reduced = reduced - alpha * back(reduced, shift) - gamma * ahead(reduced, shift)
    e_even = reduced * inv_diag
    e_odd = (bo + fo * e_even + fe_next * ahead(e_even, 1)) * inv_odd
    line_even = lax.broadcasted_iota(jnp.int32, (n, ny), 1) % 2 == 0
    xs[pl.ds(8, n), :] = jnp.where(line_even, e_even, e_odd)

    def line(k):
        return jnp.broadcast_to(xs[pl.ds(me + 8 + k, 1), :], (hx_rows, ny))

    receive(vn_up, vn_low)
    pl.when(has_low2)(far_up.wait_recv)
    pl.when(has_up2)(far_low.wait_recv)
    far_below, far_above = far_in[0], far_in[1]
    w1 = [far_below + jnp.where(pltpu.roll(far_below, 1, 1) > 0.0, line(-2), 0.0)]
    for k in range(3):
        w1.append(vn[k] + jnp.where(cof[k, 0] > 0.0, line(k - 1), 0.0))
    w1.append(far_above + jnp.where(pltpu.roll(far_above, ny - 1, 1) > 0.0, line(2), 0.0))
    w3 = coarse_sweep(coarse_sweep(w1))

    def prolong(slot, plane):
        pro[slot, pl.ds(0, hx_rows, 2), :] = plane
        pro[slot, pl.ds(1, hx_rows, 2), :] = plane

    def lower_plane(pack):
        return jnp.where(even, pack, pltpu.roll(pack, 1, 1))

    def upper_plane(pack):
        return jnp.where(even, pltpu.roll(pack, ny - 1, 1), pack)

    prolong(0, upper_plane(w3[1]))
    prolong(1, lower_plane(w3[2]))
    prolong(2, upper_plane(w3[2]))
    prolong(3, lower_plane(w3[3]))

    receive(u2_up, u2_low)

    def correct(k):
        ua[k] = ub[k] + jnp.where(idf[k] > 0.0, pro[k // 2], 0.0)

    over(0, 8, correct)

    pl.when(has_up)(u2_up.wait_send)
    pl.when(has_low)(u2_low.wait_send)
    over(1, 7, sweep(ua, tmp))
    over(2, 6, sweep(tmp, outv, 2))
    store = pltpu.make_async_copy(outv, out_hbm.at[0], load_sem.at[2])
    store.start()

    for upward, downward in (
        (lab_up, lab_low), (rhs_up, rhs_low), (cof_up, cof_low), (b1_up, b1_low), (vn_up, vn_low),
    ):
        pl.when(has_up)(upward.wait_send)
        pl.when(has_low)(downward.wait_send)
    pl.when(has_up2)(far_up.wait_send)
    pl.when(has_low2)(far_low.wait_send)
    gather_wait(line_all, 0, 0)
    gather_wait(row_all, 0, 1)
    store.wait()


def on_device(n, rhs, labels, sigma_table):
    planes, nx, ny = labels.shape
    fine = lambda count: pltpu.VMEM((count, nx, ny), jnp.float32)
    packs = lambda *counts: pltpu.VMEM((*counts, nx // 2, ny), jnp.float32)
    tiles = lambda *counts: pltpu.VMEM((*counts, 8, ny), jnp.float32)
    return pl.pallas_call(
        functools.partial(kernel, n),
        out_shape=jax.ShapeDtypeStruct(rhs.shape, jnp.float32),
        in_specs=[
            pl.BlockSpec(memory_space=pl.ANY),
            pl.BlockSpec(memory_space=pl.ANY),
            pl.BlockSpec(memory_space=pltpu.SMEM),
        ],
        out_specs=pl.BlockSpec(memory_space=pl.ANY),
        scratch_shapes=[
            pltpu.VMEM((10, nx, ny), jnp.int32),
            fine(8), fine(8), fine(8), fine(8), fine(8), fine(8), fine(8), fine(8), fine(8),
            fine(8), fine(8), fine(8), fine(4),
            packs(3, 5), packs(), packs(3), packs(3), packs(2), packs(2),
            tiles(), tiles(n), tiles(), tiles(n),
            pltpu.VMEM((n + 16, ny), jnp.float32),
            fine(4),
            pltpu.SemaphoreType.DMA((3,)),
            pltpu.SemaphoreType.DMA((2, 14)),
            pltpu.SemaphoreType.DMA((2, 2)),
        ],
        compiler_params=pltpu.CompilerParams(collective_id=0, has_side_effects=True),
    )(rhs, labels, sigma_table)


def solution(mesh):
    placed = (P("groups", "slab", None, None), P("slab", "groups", None), P())
    return jax.shard_map(
        functools.partial(on_device, mesh.shape["slab"]),
        mesh=mesh,
        in_specs=placed,
        out_specs=P("groups", "slab", None, None),
        check_vma=False,
    )
```

time: 268 us -> 32.1 us (0.12)
  the two profiles are of different devices: /device:TPU:8 before, /device:TPU:0 now
where the time goes in v1:
time: 32.1 us; the launch traced here: 31.9 us
  Pallas kernels  28.8 us (90%)
  local copies, waits for them, and re-layouts  3.02 us (9%)
    pallas_call x1, Pallas kernels, on_device(): pl.pallas_call(functools.partial(kernel, n), out_shape=jax.ShapeDtypeStru...  28.8 us
    unnamed x2, local copies, waits for them, and re-layouts  3.02 us

profile of v1, /device:TPU:0, one launch (start us, length us, event | category | flops | bytes accessed | tf_op | source)
XLA Modules:
  0.0 31.9 jit_solution(4626961750158159548)
XLA Ops:
  0.0 1.4 %copy.4.table = f32[5,3]{1,0:T(8,128)} copy(f32[5,3]{0,1:T(4,128)} %param.5) | data formatting | bytes 120 | tf_op args[2]
  1.4 28.8 %shard_map.37 = f32[1,4,128,128]{3,2,1,0:T(8,128)} custom-call(f32[1,4,128,128]{3,2,1,0:T(8,128)} %rhs_hbm.1, s32[4,128,128]{2,1,0:T(8,128)} %lab_hbm.1, f32[5,3]{1,0:T(8,128)} %copy.4.table), custom_call_target="tpu_custom_call" | custom-call | tf_op jit(solution)/shard_map/pallas_call | solution.py:403
  30.2 1.7 %copy.6 = f32[1,4,128,128]{3,2,1,0:T(8,128)} copy(f32[1,4,128,128]{3,2,1,0:T(8,128)} %shard_map.37) | data formatting | bytes 524288

commit v2 on v1

v2 whole, which is shorter than its diff:
```python
import functools

import jax
import jax.numpy as jnp
from jax import lax
from jax.experimental import pallas as pl
from jax.experimental.pallas import tpu as pltpu
from jax.sharding import PartitionSpec as P

OMEGA = 0.8
LABELS = 5
MESH = pl.DeviceIdType.MESH


def copy_to(src, dst, sems, slot, target):
    return pltpu.make_async_remote_copy(
        src_ref=src,
        dst_ref=dst,
        send_sem=sems.at[0, slot],
        recv_sem=sems.at[1, slot],
        device_id={"slab": target},
        device_id_type=MESH,
    )


def kernel(
    n, rhs_hbm, lab_hbm, table_hbm, out_hbm,
    lab, rhs, gx, gxr, gy, gyr, gzl, gzh, idf, dg, ua, ub, tmp, pro,
    cof, d1, b1, vn, line_out, line_all, row_out, row_all, xs, outv, table,
    load_sem, sems, gather_sem,
):
    me = lax.axis_index("slab")
    nx, ny = lab.shape[1:]
    hx_rows = nx // 2
    has_low, has_up = me > 0, me < n - 1

    load_table = pltpu.make_async_copy(table_hbm, table, load_sem.at[3])
    load_table.start()
    barrier = pltpu.get_barrier_semaphore()

    def greet(step, carry):
        other = lax.rem(me + step, n)
        pl.semaphore_signal(barrier, inc=1, device_id={"slab": other}, device_id_type=MESH)
        return carry

    lax.fori_loop(1, n, greet, 0)
    pl.semaphore_wait(barrier, n - 1)

    up, low = lax.rem(me + 1, n), lax.rem(me + n - 1, n)
    near_up = copy_to(lab_hbm.at[3], lab.at[1], sems, 0, up)
    near_low = copy_to(lab_hbm.at[0], lab.at[6], sems, 1, low)
    next_up = copy_to(lab_hbm.at[2], lab.at[0], sems, 2, up)
    next_low = copy_to(lab_hbm.at[1], lab.at[7], sems, 3, low)
    rhs_up = copy_to(rhs_hbm.at[0, 3], rhs.at[1], sems, 4, up)
    rhs_low = copy_to(rhs_hbm.at[0, 0], rhs.at[6], sems, 5, low)
    u1_up = copy_to(ua.at[4], ua.at[0], sems, 6, up)
    u1_low = copy_to(ua.at[3], ua.at[7], sems, 7, low)
    cof_up = copy_to(cof.at[1, pl.ds(0, 4)], cof.at[0, pl.ds(0, 4)], sems, 8, up)
    cof_low = copy_to(cof.at[1, pl.ds(1, 4)], cof.at[2, pl.ds(1, 4)], sems, 9, low)
    b1_up = copy_to(b1.at[1], b1.at[0], sems, 10, up)
    b1_low = copy_to(b1.at[1], b1.at[2], sems, 11, low)
    u2_up = copy_to(ub.at[4], ub.at[0], sems, 12, up)
    u2_low = copy_to(ub.at[3], ub.at[7], sems, 13, low)
    vn_up = copy_to(vn.at[1], vn.at[0], sems, 14, up)
    vn_low = copy_to(vn.at[1], vn.at[2], sems, 15, low)

    def send(upward, downward):
        pl.when(has_up)(upward.start)
        pl.when(has_low)(downward.start)

    def receive(upward, downward):
        pl.when(has_low)(upward.wait_recv)
        pl.when(has_up)(downward.wait_recv)

    send(near_up, near_low)
    own_lab = pltpu.make_async_copy(lab_hbm, lab.at[pl.ds(2, 4)], load_sem.at[0])
    own_rhs = pltpu.make_async_copy(rhs_hbm.at[0], rhs.at[pl.ds(2, 4)], load_sem.at[1])
    own_lab.start()
    own_rhs.start()
    send(next_up, next_low)
    send(rhs_up, rhs_low)

    def clear(ref, first, count):
        for k in range(first, first + count):
            ref[k] = jnp.zeros(ref.shape[1:], ref.dtype)

    @pl.when(me == 0)
    def _():
        clear(lab, 0, 2)
        clear(rhs, 1, 1)
        clear(ua, 0, 1)
        clear(cof.at[0], 0, 4)
        clear(b1, 0, 1)
        clear(ub, 0, 1)
        clear(vn, 0, 1)

    @pl.when(me == n - 1)
    def _():
        clear(lab, 6, 2)
        clear(rhs, 6, 1)
        clear(ua, 7, 1)
        clear(cof.at[2], 1, 4)
        clear(b1, 2, 1)
        clear(ub, 7, 1)
        clear(vn, 2, 1)

    xs[...] = jnp.zeros(xs.shape, xs.dtype)

    fine_row = lax.broadcasted_iota(jnp.int32, (nx, ny), 0) % 2 == 1
    fine_lane = lax.broadcasted_iota(jnp.int32, (nx, ny), 1) % 2 == 1
    even = lax.broadcasted_iota(jnp.int32, (hx_rows, ny), 1) % 2 == 0

    def select(values, column):
        chosen = jnp.full(values.shape, table[column, 0], jnp.float32)
        for tissue in range(1, LABELS):
            chosen = jnp.where(values == tissue, table[column, tissue], chosen)
        return chosen

    def harmonic(a, b):
        return 2.0 * a * b / (a + b)

    def plane_terms(k):
        here, below, above = lab[k], lab[k - 1], lab[k + 1]
        a = (here > 0).astype(jnp.float32)
        sx, sy, sz = select(here, 0), select(here, 1), select(here, 2)
        hx = harmonic(pltpu.roll(sx, 1, 0), sx)
        faces = hx + pltpu.roll(hx, nx - 1, 0)
        cx = hx * a * pltpu.roll(a, 1, 0)
        gx[k] = cx
        gxr[k] = pltpu.roll(cx, nx - 1, 0)
        hy = harmonic(pltpu.roll(sy, 1, 1), sy)
        faces = faces + hy + pltpu.roll(hy, ny - 1, 1)
        cy = hy * a * pltpu.roll(a, 1, 1)
        gy[k] = cy
        gyr[k] = pltpu.roll(cy, ny - 1, 1)
        hl = harmonic(select(below, 2), sz)
        gzl[k] = hl * a * (below > 0).astype(jnp.float32)
        hh = harmonic(sz, select(above, 2))
        gzh[k] = hh * a * (above > 0).astype(jnp.float32)
        faces = faces + hl + hh
        diagonal = a * faces + (1.0 - a)
        dg[k] = diagonal
        idf[k] = OMEGA * a / diagonal

    def over(first, last, body):
        def step(k, carry):
            body(k)
            return carry

        lax.fori_loop(first, last, step, 0)

    def first_sweep(k):
        ua[k] = idf[k] * rhs[k]

    load_table.wait()
    own_lab.wait()
    over(3, 5, plane_terms)
    own_rhs.wait()
    over(3, 5, first_sweep)
    send(u1_up, u1_low)

    receive(near_up, near_low)
    over(0, 2, lambda k: plane_terms(2 + 3 * k))
    over(0, 2, lambda k: first_sweep(2 + 3 * k))

    def rows_even(plane):
        tmp[0] = plane
        return tmp[0, pl.ds(0, hx_rows, 2), :]

    def rows_sum(plane):
        tmp[0] = plane
        return tmp[0, pl.ds(0, hx_rows, 2), :] + tmp[0, pl.ds(1, hx_rows, 2), :]

    def lanes_sum(t0, t1):
        return jnp.where(even, t0 + pltpu.roll(t0, ny - 1, 1), t1 + pltpu.roll(t1, 1, 1))

    def lanes_even(t0, t1):
        return jnp.where(even, t0, pltpu.roll(t1, 1, 1))

    def restrict(p0, p1):
        return lanes_sum(rows_sum(p0), rows_sum(p1))

    def inner(k):
        mask = (idf[k] > 0.0).astype(jnp.float32)
        doubled = jnp.where(fine_row, gx[k], 0.0) + jnp.where(fine_lane, gy[k], 0.0)
        if k % 2 == 1:
            doubled = doubled + gzl[k]
        return mask * dg[k] - 2.0 * doubled, mask

    (f0, m0), (f1, m1), (f2, m2), (f3, m3) = inner(2), inner(3), inner(4), inner(5)
    raw = restrict(f0 + f1, f2 + f3)
    active1 = jnp.minimum(restrict(m0 + m1, m2 + m3), 1.0)
    diag1 = raw + (1.0 - active1)
    d1[...] = diag1
    cof[1, 1] = OMEGA * active1 / diag1
    coarse_x = lanes_sum(rows_even(gx[2] + gx[3]), rows_even(gx[4] + gx[5]))
    coarse_y = lanes_even(rows_sum(gy[2] + gy[3]), rows_sum(gy[4] + gy[5]))
    coarse_zl = restrict(gzl[2], gzl[4])
    cof[1, 2] = coarse_x
    cof[1, 3] = coarse_y
    cof[1, 0] = coarse_zl
    cof[1, 4] = restrict(gzh[3], gzh[5])
    send(cof_up, cof_low)

    def plane_sums(packed):
        lower = jnp.sum(jnp.where(even, packed, 0.0), axis=0, keepdims=True)
        upper = jnp.sum(jnp.where(even, 0.0, packed), axis=0, keepdims=True)
        lower = jnp.sum(lower, axis=1, keepdims=True)
        upper = jnp.sum(upper, axis=1, keepdims=True)
        return lower, upper

    sub = lax.broadcasted_iota(jnp.int32, (8, ny), 0)

    sub_even = lax.broadcasted_iota(jnp.int32, (8, ny), 1) % 2 == 0

    def gather(out, everyone, slot, pairs):
        tile = jnp.zeros((8, ny), jnp.float32)
        for row, (lower, upper) in enumerate(pairs):
            tile = jnp.where(sub == row, jnp.where(sub_even, lower, upper), tile)
        out[...] = tile
        everyone[me] = tile
        rows = pl.ds(0, len(pairs))

        def one(step, carry):
            pltpu.make_async_remote_copy(
                src_ref=out.at[rows],
                dst_ref=everyone.at[me, rows],
                send_sem=gather_sem.at[0, slot],
                recv_sem=gather_sem.at[1, slot],
                device_id={"slab": lax.rem(me + step, n)},
                device_id_type=MESH,
            ).start()
            return carry

        lax.fori_loop(1, n, one, 0)

    def gather_wait(everyone, side, slot, count):
        rest = everyone.at[pl.ds(0, n - 1), pl.ds(0, count)]
        pltpu.make_async_copy(rest, rest, gather_sem.at[side, slot]).wait()

    line_diag = plane_sums(raw - 2.0 * (coarse_x + coarse_y))
    gather(line_out, line_all, 0, (line_diag, plane_sums(coarse_zl)))

    receive(next_up, next_low)
    over(0, 2, lambda k: plane_terms(1 + 5 * k))
    receive(rhs_up, rhs_low)
    over(0, 2, lambda k: first_sweep(1 + 5 * k))
    receive(u1_up, u1_low)

    def neighbours(field, k):
        u = field[k]
        total = gx[k] * pltpu.roll(u, 1, 0) + gxr[k] * pltpu.roll(u, nx - 1, 0)
        total = total + gy[k] * pltpu.roll(u, 1, 1) + gyr[k] * pltpu.roll(u, ny - 1, 1)
        return u, total + gzl[k] * field[k - 1] + gzh[k] * field[k + 1]

    def sweep(src, dst, shift=0):
        def body(k):
            u, total = neighbours(src, k)
            dst[k - shift] = (1.0 - OMEGA) * u + idf[k] * (rhs[k] + total)

        return body

    over(1, 7, sweep(ua, ub))

    def residual(k):
        u, total = neighbours(ub, k)
        return jnp.where(idf[k] > 0.0, rhs[k] - dg[k] * u + total, 0.0)

    b1[1] = restrict(residual(2) + residual(3), residual(4) + residual(5))
    send(b1_up, b1_low)
    send(u2_up, u2_low)

    gather_wait(line_all, 1, 0, 2)

    line_even = lax.broadcasted_iota(jnp.int32, (n, ny), 1) % 2 == 0

    def line_rows(everyone, row):
        both = everyone.reshape(n * 8, ny)[pl.ds(row, n, 8), :]
        lower = jnp.where(line_even, both, pltpu.roll(both, 1, 1))
        return lower, jnp.where(line_even, pltpu.roll(both, ny - 1, 1), both)

    (de, do), (fe, fo) = line_rows(line_all, 0), line_rows(line_all, 1)

    def back(x, s):
        return pltpu.roll(x, s % n, 0)

    def ahead(x, s):
        return pltpu.roll(x, (n - s) % n, 0)

    inv_odd = 1.0 / do
    to_low = fe * back(inv_odd, 1)
    to_up = fo * inv_odd
    fe_next = ahead(fe, 1)
    diag = de - fe * to_low - fo * to_up
    lower = -to_low * back(fo, 1)
    upper = -to_up * fe_next
    steps = []
    shift = 1
    while shift < n:
        alpha, gamma = lower / back(diag, shift), upper / ahead(diag, shift)
        steps.append((shift, alpha, gamma))
        diag = diag - alpha * back(upper, shift) - gamma * ahead(lower, shift)
        lower, upper = -alpha * back(lower, shift), -gamma * ahead(upper, shift)
        shift *= 2
    inv_diag = 1.0 / diag

    receive(cof_up, cof_low)
    cof[0, 4] = jnp.where(even, pltpu.roll(cof[0, 0], ny - 1, 1), pltpu.roll(cof[1, 0], 1, 1))
    cof[2, 0] = jnp.where(even, pltpu.roll(cof[1, 4], ny - 1, 1), pltpu.roll(cof[2, 4], 1, 1))
    receive(b1_up, b1_low)

    zero = jnp.zeros((hx_rows, ny), jnp.float32)

    def coarse_neighbours(k, below, f, above):
        cx, cy = cof[k, 2], cof[k, 3]
        zl = jnp.where(even, pltpu.roll(below, ny - 1, 1), pltpu.roll(f, 1, 1))
        zh = jnp.where(even, pltpu.roll(f, ny - 1, 1), pltpu.roll(above, 1, 1))
        total = cx * pltpu.roll(f, 1, 0)
        total = total + pltpu.roll(cx, hx_rows - 1, 0) * pltpu.roll(f, hx_rows - 1, 0)
        total = total + cy * pltpu.roll(f, 2, 1)
        total = total + pltpu.roll(cy, ny - 2, 1) * pltpu.roll(f, ny - 2, 1)
        return total + cof[k, 0] * zl + cof[k, 4] * zh

    def coarse_sweep(fields):
        swept = []
        for k in range(3):
            total = coarse_neighbours(k, fields[k], fields[k + 1], fields[k + 2])
            swept.append((1.0 - OMEGA) * fields[k + 1] + cof[k, 1] * (b1[k] + total))
        return [zero] + swept + [zero]

    v1 = [zero] + [cof[k, 1] * b1[k] for k in range(3)] + [zero]
    v2 = coarse_sweep(v1)
    own_total = coarse_neighbours(1, v2[1], v2[2], v2[3])
    r1 = jnp.where(cof[1, 1] > 0.0, b1[1] - d1[...] * v2[2] + own_total, 0.0)
    gather(row_out, row_all, 1, (plane_sums(r1),))
    vn[1] = (1.0 - OMEGA) * v2[2] + cof[1, 1] * (b1[1] + own_total)
    send(vn_up, vn_low)

    parts = []
    for k in range(3):
        weight, cx, cy = cof[k, 1], cof[k, 2], cof[k, 3]
        around = cx + pltpu.roll(cx, hx_rows - 1, 0) + cy + pltpu.roll(cy, ny - 2, 1)
        own_part = jnp.where(weight > 0.0, 1.0 - OMEGA, 0.0) + weight * around
        parts.append((own_part, weight * cof[k, 0], weight * cof[k, 4]))
    receive(vn_up, vn_low)

    gather_wait(row_all, 1, 1, 1)
    be, bo = line_rows(row_all, 0)
    reduced = be + to_low * back(bo, 1) + to_up * bo
    for shift, alpha, gamma in steps:
        reduced = reduced - alpha * back(reduced, shift) - gamma * ahead(reduced, shift)
    e_even = reduced * inv_diag
    e_odd = (bo + fo * e_even + fe_next * ahead(e_even, 1)) * inv_odd
    packed = jnp.where(line_even, e_even, e_odd)
    xs[0, pl.ds(8, n), :] = packed
    xs[1, pl.ds(8, n), :] = jnp.where(line_even, back(e_odd, 1), e_even)
    xs[2, pl.ds(8, n), :] = jnp.where(line_even, e_odd, ahead(e_even, 1))

    def line(slot, k):
        return jnp.broadcast_to(xs[slot, pl.ds(me + 7 + k, 1), :], (hx_rows, ny))

    w2 = [zero]
    for k, (own_part, lower_part, upper_part) in enumerate(parts):
        fixed = own_part * line(0, k) + lower_part * line(1, k) + upper_part * line(2, k)
        w2.append(vn[k] + fixed)
    w3 = coarse_sweep(w2 + [zero])

    def prolong(slot, plane):
        pro[slot, pl.ds(0, hx_rows, 2), :] = plane
        pro[slot, pl.ds(1, hx_rows, 2), :] = plane

    def lower_plane(pack):
        return jnp.where(even, pack, pltpu.roll(pack, 1, 1))

    def upper_plane(pack):
        return jnp.where(even, pltpu.roll(pack, ny - 1, 1), pack)

    prolong(0, upper_plane(w3[1]))
    prolong(1, lower_plane(w3[2]))
    prolong(2, upper_plane(w3[2]))
    prolong(3, lower_plane(w3[3]))

    receive(u2_up, u2_low)

    def correct(k):
        ua[k] = ub[k] + jnp.where(lab[k] > 0, pro[k // 2], 0.0)

    pl.when(has_up)(u1_up.wait_send)
    pl.when(has_low)(u1_low.wait_send)
    over(0, 8, correct)

    over(1, 7, sweep(ua, tmp))
    over(2, 6, sweep(tmp, outv, 2))
    store = pltpu.make_async_copy(outv, out_hbm.at[0], load_sem.at[2])
    store.start()

    for upward, downward in (
        (near_up, near_low), (next_up, next_low), (rhs_up, rhs_low), (cof_up, cof_low), (b1_up, b1_low), (vn_up, vn_low),
        (u2_up, u2_low),
    ):
        pl.when(has_up)(upward.wait_send)
        pl.when(has_low)(downward.wait_send)
    gather_wait(line_all, 0, 0, 2)
    gather_wait(row_all, 0, 1, 1)
    store.wait()


def on_device(n, rhs, labels, sigma_table):
    planes, nx, ny = labels.shape
    fine = lambda count: pltpu.VMEM((count, nx, ny), jnp.float32)
    packs = lambda *counts: pltpu.VMEM((*counts, nx // 2, ny), jnp.float32)
    tiles = lambda *counts: pltpu.VMEM((*counts, 8, ny), jnp.float32)
    return pl.pallas_call(
        functools.partial(kernel, n),
        out_shape=jax.ShapeDtypeStruct(rhs.shape, jnp.float32),
        in_specs=[
            pl.BlockSpec(memory_space=pl.ANY),
            pl.BlockSpec(memory_space=pl.ANY),
            pl.BlockSpec(memory_space=pl.ANY),
        ],
        out_specs=pl.BlockSpec(memory_space=pl.ANY),
        scratch_shapes=[
            pltpu.VMEM((8, nx, ny), jnp.int32),
            fine(8), fine(8), fine(8), fine(8), fine(8), fine(8), fine(8), fine(8), fine(8),
            fine(8), fine(8), fine(8), fine(4),
            packs(3, 5), packs(), packs(3), packs(3),
            tiles(), tiles(n), tiles(), tiles(n),
            pltpu.VMEM((3, n + 16, ny), jnp.float32),
            fine(4),
            pltpu.SMEM((3, LABELS), jnp.float32),
            pltpu.SemaphoreType.DMA((4,)),
            pltpu.SemaphoreType.DMA((2, 16)),
            pltpu.SemaphoreType.DMA((2, 2)),
        ],
        compiler_params=pltpu.CompilerParams(collective_id=0, has_side_effects=True),
    )(rhs, labels, sigma_table.T)


def solution(mesh):
    placed = (P("groups", "slab", None, None), P("slab", "groups", None), P())
    return jax.shard_map(
        functools.partial(on_device, mesh.shape["slab"]),
        mesh=mesh,
        in_specs=placed,
        out_specs=P("groups", "slab", None, None),
        check_vma=False,
    )
```

time: 32.1 us -> 27.3 us (0.85)
  Pallas kernels: 28.8 us -> 25.4 us
  local copies, waits for them, and re-layouts: 3.02 us -> 1.67 us
    pallas_call x1, Pallas kernels: 28.8 us -> 25.4 us  [on_device(): pl.pallas_call(functools.partial(kernel, n), out_shape=jax.ShapeDtypeStru...]
    unnamed x2 -> x1, local copies, waits for them, and re-layouts: 3.02 us -> 1.67 us
where the time goes in v2:
time: 27.3 us; the launch traced here: 27.1 us
  Pallas kernels  25.4 us (93%)
  local copies, waits for them, and re-layouts  1.67 us (6%)
    pallas_call x1, Pallas kernels, on_device(): pl.pallas_call(functools.partial(kernel, n), out_shape=jax.ShapeDtypeStru...  25.4 us
    unnamed x1, local copies, waits for them, and re-layouts  1.67 us

profile of v2, /device:TPU:0, one launch (start us, length us, event | category | flops | bytes accessed | tf_op | source)
XLA Modules:
  0.0 27.1 jit_solution(7665265641656048028)
XLA Ops:
  0.0 25.4 %shard_map.37 = f32[1,4,128,128]{3,2,1,0:T(8,128)} custom-call(f32[1,4,128,128]{3,2,1,0:T(8,128)} %rhs_hbm.1, s32[4,128,128]{2,1,0:T(8,128)} %lab_hbm.1, f32[3,5]{1,0:T(4,128)} %bitcast.1), custom_call_target="tpu_custom_call" | custom-call | tf_op jit(solution)/shard_map/pallas_call | solution.py:413
  25.4 1.7 %copy.5 = f32[1,4,128,128]{3,2,1,0:T(8,128)} copy(f32[1,4,128,128]{3,2,1,0:T(8,128)} %shard_map.37) | data formatting | bytes 524288

commit v3 on v2

--- a/solution.py
+++ b/solution.py
@@ -24,9 +24,9 @@
 
 
 def kernel(
-    n, rhs_hbm, lab_hbm, table_hbm, out_hbm,
-    lab, rhs, gx, gxr, gy, gyr, gzl, gzh, idf, dg, ua, ub, tmp, pro,
-    cof, d1, b1, vn, line_out, line_all, row_out, row_all, xs, outv, table,
+    n, rhs_hbm, lab_hbm, table_hbm, out,
+    lab, rhs, gx, gy, gzl, gzh, idf, dg, ua, ub, tmp, pro,
+    cof, d1, b1, vn, line_out, line_all, row_out, row_all, xs, table,
     load_sem, sems, gather_sem,
 ):
     me = lax.axis_index("slab")
@@ -34,7 +34,7 @@
     hx_rows = nx // 2
     has_low, has_up = me > 0, me < n - 1
 
-    load_table = pltpu.make_async_copy(table_hbm, table, load_sem.at[3])
+    load_table = pltpu.make_async_copy(table_hbm, table, load_sem.at[2])
     load_table.start()
     barrier = pltpu.get_barrier_semaphore()
 
@@ -127,12 +127,10 @@
         faces = hx + pltpu.roll(hx, nx - 1, 0)
         cx = hx * a * pltpu.roll(a, 1, 0)
         gx[k] = cx
-        gxr[k] = pltpu.roll(cx, nx - 1, 0)
         hy = harmonic(pltpu.roll(sy, 1, 1), sy)
         faces = faces + hy + pltpu.roll(hy, ny - 1, 1)
         cy = hy * a * pltpu.roll(a, 1, 1)
         gy[k] = cy
-        gyr[k] = pltpu.roll(cy, ny - 1, 1)
         hl = harmonic(select(below, 2), sz)
         gzl[k] = hl * a * (below > 0).astype(jnp.float32)
         hh = harmonic(sz, select(above, 2))
@@ -143,14 +141,31 @@
         idf[k] = OMEGA * a / diagonal
 
     def over(first, last, body):
-        def step(k, carry):
+        for k in range(first, last):
             body(k)
-            return carry
-
-        lax.fori_loop(first, last, step, 0)
 
     def first_sweep(k):
         ua[k] = idf[k] * rhs[k]
+
+    def neighbours(field, k):
+        u = field[k]
+        cx, cy = gx[k], gy[k]
+        total = cx * pltpu.roll(u, 1, 0) + pltpu.roll(cx * u, nx - 1, 0)
+        total = total + cy * pltpu.roll(u, 1, 1) + pltpu.roll(cy * u, ny - 1, 1)
+        return u, total + gzl[k] * field[k - 1] + gzh[k] * field[k + 1]
+
+    def sweep(src, dst, shift=0):
+        def body(k):
+            u, total = neighbours(src, k)
+            dst[k - shift] = (1.0 - OMEGA) * u + idf[k] * (rhs[k] + total)
+
+        return body
+
+    def residual(k):
+        u, total = neighbours(ub, k)
+        return jnp.where(idf[k] > 0.0, rhs[k] - dg[k] * u + total, 0.0)
+
+    second_sweep = sweep(ua, ub)
 
     load_table.wait()
     own_lab.wait()
@@ -241,32 +256,16 @@
     line_diag = plane_sums(raw - 2.0 * (coarse_x + coarse_y))
     gather(line_out, line_all, 0, (line_diag, plane_sums(coarse_zl)))
 
+    over(3, 5, second_sweep)
     receive(next_up, next_low)
     over(0, 2, lambda k: plane_terms(1 + 5 * k))
     receive(rhs_up, rhs_low)
     over(0, 2, lambda k: first_sweep(1 + 5 * k))
+    over(0, 2, lambda k: second_sweep(2 + 3 * k))
+    r3, r4 = residual(3), residual(4)
     receive(u1_up, u1_low)
-
-    def neighbours(field, k):
-        u = field[k]
-        total = gx[k] * pltpu.roll(u, 1, 0) + gxr[k] * pltpu.roll(u, nx - 1, 0)
-        total = total + gy[k] * pltpu.roll(u, 1, 1) + gyr[k] * pltpu.roll(u, ny - 1, 1)
-        return u, total + gzl[k] * field[k - 1] + gzh[k] * field[k + 1]
-
-    def sweep(src, dst, shift=0):
-        def body(k):
-            u, total = neighbours(src, k)
-            dst[k - shift] = (1.0 - OMEGA) * u + idf[k] * (rhs[k] + total)
-
-        return body
-
-    over(1, 7, sweep(ua, ub))
-
-    def residual(k):
-        u, total = neighbours(ub, k)
-        return jnp.where(idf[k] > 0.0, rhs[k] - dg[k] * u + total, 0.0)
-
-    b1[1] = restrict(residual(2) + residual(3), residual(4) + residual(5))
+    over(0, 2, lambda k: second_sweep(1 + 5 * k))
+    b1[1] = restrict(residual(2) + r3, r4 + residual(5))
     send(b1_up, b1_low)
     send(u2_up, u2_low)
 
@@ -316,9 +315,9 @@
         zl = jnp.where(even, pltpu.roll(below, ny - 1, 1), pltpu.roll(f, 1, 1))
         zh = jnp.where(even, pltpu.roll(f, ny - 1, 1), pltpu.roll(above, 1, 1))
         total = cx * pltpu.roll(f, 1, 0)
-        total = total + pltpu.roll(cx, hx_rows - 1, 0) * pltpu.roll(f, hx_rows - 1, 0)
+        total = total + pltpu.roll(cx * f, hx_rows - 1, 0)
         total = total + cy * pltpu.roll(f, 2, 1)
-        total = total + pltpu.roll(cy, ny - 2, 1) * pltpu.roll(f, ny - 2, 1)
+        total = total + pltpu.roll(cy * f, ny - 2, 1)
         return total + cof[k, 0] * zl + cof[k, 4] * zh
 
     def coarse_sweep(fields):
@@ -390,9 +389,7 @@
     over(0, 8, correct)
 
     over(1, 7, sweep(ua, tmp))
-    over(2, 6, sweep(tmp, outv, 2))
-    store = pltpu.make_async_copy(outv, out_hbm.at[0], load_sem.at[2])
-    store.start()
+    over(2, 6, sweep(tmp, out.at[0], 2))
 
     for upward, downward in (
         (near_up, near_low), (next_up, next_low), (rhs_up, rhs_low), (cof_up, cof_low), (b1_up, b1_low), (vn_up, vn_low),
@@ -402,7 +399,6 @@
         pl.when(has_low)(downward.wait_send)
     gather_wait(line_all, 0, 0, 2)
     gather_wait(row_all, 0, 1, 1)
-    store.wait()
 
 
 def on_device(n, rhs, labels, sigma_table):
@@ -412,23 +408,22 @@
     tiles = lambda *counts: pltpu.VMEM((*counts, 8, ny), jnp.float32)
     return pl.pallas_call(
         functools.partial(kernel, n),
-        out_shape=jax.ShapeDtypeStruct(rhs.shape, jnp.float32),
+        out_shape=pltpu.VMEM(rhs.shape, jnp.float32),
         in_specs=[
             pl.BlockSpec(memory_space=pl.ANY),
             pl.BlockSpec(memory_space=pl.ANY),
             pl.BlockSpec(memory_space=pl.ANY),
         ],
-        out_specs=pl.BlockSpec(memory_space=pl.ANY),
+        out_specs=pl.BlockSpec(memory_space=pltpu.VMEM),
         scratch_shapes=[
             pltpu.VMEM((8, nx, ny), jnp.int32),
             fine(8), fine(8), fine(8), fine(8), fine(8), fine(8), fine(8), fine(8), fine(8),
-            fine(8), fine(8), fine(8), fine(4),
+            fine(8), fine(4),
             packs(3, 5), packs(), packs(3), packs(3),
             tiles(), tiles(n), tiles(), tiles(n),
             pltpu.VMEM((3, n + 16, ny), jnp.float32),
-            fine(4),
             pltpu.SMEM((3, LABELS), jnp.float32),
-            pltpu.SemaphoreType.DMA((4,)),
+            pltpu.SemaphoreType.DMA((3,)),
             pltpu.SemaphoreType.DMA((2, 16)),
             pltpu.SemaphoreType.DMA((2, 2)),
         ],

time: 27.3 us -> 24.2 us (0.89)
  Pallas kernels: 25.4 us -> 23.4 us
  local copies, waits for them, and re-layouts: 1.67 us -> 0.71 us
    pallas_call x1, Pallas kernels: 25.4 us -> 23.4 us  [on_device(): pl.pallas_call(functools.partial(kernel, n), out_shape=pltpu.VMEM(rhs.sha...]
    unnamed x1, local copies, waits for them, and re-layouts: 1.67 us -> 0.71 us
where the time goes in v3:
time: 24.2 us; the launch traced here: 24.1 us
  Pallas kernels  23.4 us (97%)
  local copies, waits for them, and re-layouts  0.71 us (3%)
    pallas_call x1, Pallas kernels, on_device(): pl.pallas_call(functools.partial(kernel, n), out_shape=pltpu.VMEM(rhs.sha...  23.4 us
    unnamed x1, local copies, waits for them, and re-layouts  0.71 us

profile of v3, /device:TPU:0, one launch (start us, length us, event | category | flops | bytes accessed | tf_op | source)
XLA Modules:
  0.0 24.1 jit_solution(15050125580770054503)
XLA Ops:
  0.0 23.4 %shard_map.37 = f32[1,4,128,128]{3,2,1,0:T(8,128)S(1)} custom-call(f32[1,4,128,128]{3,2,1,0:T(8,128)} %rhs_hbm.1, s32[4,128,128]{2,1,0:T(8,128)} %lab_hbm.1, f32[3,5]{1,0:T(4,128)} %bitcast.1), custom_call_target="tpu_custom_call" | custom-call | tf_op jit(solution)/shard_map/pallas_call | solution.py:409
  23.4 0.7 %copy.5 = f32[1,4,128,128]{3,2,1,0:T(8,128)} copy(f32[1,4,128,128]{3,2,1,0:T(8,128)S(1)} %shard_map.37) | data formatting | bytes 524288

commit v4 on v3

--- a/solution.py
+++ b/solution.py
@@ -27,7 +27,7 @@
     n, rhs_hbm, lab_hbm, table_hbm, out,
     lab, rhs, gx, gy, gzl, gzh, idf, dg, ua, ub, tmp, pro,
     cof, d1, b1, vn, line_out, line_all, row_out, row_all, xs, table,
-    load_sem, sems, gather_sem,
+    load_sem, sems, gather_sem, tokens,
 ):
     me = lax.axis_index("slab")
     nx, ny = lab.shape[1:]
@@ -38,15 +38,34 @@
     load_table.start()
     barrier = pltpu.get_barrier_semaphore()
 
-    def greet(step, carry):
-        other = lax.rem(me + step, n)
-        pl.semaphore_signal(barrier, inc=1, device_id={"slab": other}, device_id_type=MESH)
-        return carry
-
-    lax.fori_loop(1, n, greet, 0)
-    pl.semaphore_wait(barrier, n - 1)
-
     up, low = lax.rem(me + 1, n), lax.rem(me + n - 1, n)
+
+    def greet(sem, distance):
+        for near, other in ((me >= distance, me - distance), (me + distance < n, me + distance)):
+
+            @pl.when(near)
+            def _():
+                pl.semaphore_signal(sem, inc=1, device_id={"slab": other}, device_id_type=MESH)
+
+    def greeted(sem, distance):
+        both = jnp.logical_and(me >= distance, me + distance < n)
+        one = jnp.logical_xor(me >= distance, me + distance < n)
+        pl.when(both)(lambda: pl.semaphore_wait(sem, 2))
+        pl.when(one)(lambda: pl.semaphore_wait(sem, 1))
+
+    greet(barrier, 1)
+    greeted(barrier, 1)
+
+    rounds = [2**r for r in range((n - 1).bit_length())]
+
+    def round_start(r):
+        if r < len(rounds):
+            greet(tokens.at[r], rounds[r])
+
+    def round_end(r):
+        if r < len(rounds):
+            greeted(tokens.at[r], rounds[r])
+
     near_up = copy_to(lab_hbm.at[3], lab.at[1], sems, 0, up)
     near_low = copy_to(lab_hbm.at[0], lab.at[6], sems, 1, low)
     next_up = copy_to(lab_hbm.at[2], lab.at[0], sems, 2, up)
@@ -79,6 +98,7 @@
     own_rhs.start()
     send(next_up, next_low)
     send(rhs_up, rhs_low)
+    round_start(0)
 
     def clear(ref, first, count):
         for k in range(first, first + count):
@@ -175,6 +195,8 @@
     send(u1_up, u1_low)
 
     receive(near_up, near_low)
+    round_end(0)
+    round_start(1)
     over(0, 2, lambda k: plane_terms(2 + 3 * k))
     over(0, 2, lambda k: first_sweep(2 + 3 * k))
 
@@ -254,12 +276,16 @@
         pltpu.make_async_copy(rest, rest, gather_sem.at[side, slot]).wait()
 
     line_diag = plane_sums(raw - 2.0 * (coarse_x + coarse_y))
-    gather(line_out, line_all, 0, (line_diag, plane_sums(coarse_zl)))
+    line_face = plane_sums(coarse_zl)
 
     over(3, 5, second_sweep)
     receive(next_up, next_low)
+    round_end(1)
+    round_start(2)
     over(0, 2, lambda k: plane_terms(1 + 5 * k))
     receive(rhs_up, rhs_low)
+    round_end(2)
+    round_start(3)
     over(0, 2, lambda k: first_sweep(1 + 5 * k))
     over(0, 2, lambda k: second_sweep(2 + 3 * k))
     r3, r4 = residual(3), residual(4)
@@ -268,6 +294,49 @@
     b1[1] = restrict(residual(2) + r3, r4 + residual(5))
     send(b1_up, b1_low)
     send(u2_up, u2_low)
+    for r in range(3, len(rounds)):
+        round_end(r)
+        round_start(r + 1)
+    gather(line_out, line_all, 0, (line_diag, line_face))
+
+    receive(cof_up, cof_low)
+    cof[0, 4] = jnp.where(even, pltpu.roll(cof[0, 0], ny - 1, 1), pltpu.roll(cof[1, 0], 1, 1))
+    cof[2, 0] = jnp.where(even, pltpu.roll(cof[1, 4], ny - 1, 1), pltpu.roll(cof[2, 4], 1, 1))
+    receive(b1_up, b1_low)
+
+    zero = jnp.zeros((hx_rows, ny), jnp.float32)
+
+    def coarse_neighbours(k, below, f, above):
+        cx, cy = cof[k, 2], cof[k, 3]
+        zl = jnp.where(even, pltpu.roll(below, ny - 1, 1), pltpu.roll(f, 1, 1))
+        zh = jnp.where(even, pltpu.roll(f, ny - 1, 1), pltpu.roll(above, 1, 1))
+        total = cx * pltpu.roll(f, 1, 0)
+        total = total + pltpu.roll(cx * f, hx_rows - 1, 0)
+        total = total + cy * pltpu.roll(f, 2, 1)
+        total = total + pltpu.roll(cy * f, ny - 2, 1)
+        return total + cof[k, 0] * zl + cof[k, 4] * zh
+
+    def coarse_sweep(fields):
+        swept = []
+        for k in range(3):
+            total = coarse_neighbours(k, fields[k], fields[k + 1], fields[k + 2])
+            swept.append((1.0 - OMEGA) * fields[k + 1] + cof[k, 1] * (b1[k] + total))
+        return [zero] + swept + [zero]
+
+    v1 = [zero] + [cof[k, 1] * b1[k] for k in range(3)] + [zero]
+    v2 = coarse_sweep(v1)
+    own_total = coarse_neighbours(1, v2[1], v2[2], v2[3])
+    r1 = jnp.where(cof[1, 1] > 0.0, b1[1] - d1[...] * v2[2] + own_total, 0.0)
+    gather(row_out, row_all, 1, (plane_sums(r1),))
+    vn[1] = (1.0 - OMEGA) * v2[2] + cof[1, 1] * (b1[1] + own_total)
+    send(vn_up, vn_low)
+
+    parts = []
+    for k in range(3):
+        weight, cx, cy = cof[k, 1], cof[k, 2], cof[k, 3]
+        around = cx + pltpu.roll(cx, hx_rows - 1, 0) + cy + pltpu.roll(cy, ny - 2, 1)
+        own_part = jnp.where(weight > 0.0, 1.0 - OMEGA, 0.0) + weight * around
+        parts.append((own_part, weight * cof[k, 0], weight * cof[k, 4]))
 
     gather_wait(line_all, 1, 0, 2)
 
@@ -303,46 +372,7 @@
         shift *= 2
     inv_diag = 1.0 / diag
 
-    receive(cof_up, cof_low)
-    cof[0, 4] = jnp.where(even, pltpu.roll(cof[0, 0], ny - 1, 1), pltpu.roll(cof[1, 0], 1, 1))
-    cof[2, 0] = jnp.where(even, pltpu.roll(cof[1, 4], ny - 1, 1), pltpu.roll(cof[2, 4], 1, 1))
-    receive(b1_up, b1_low)
-
-    zero = jnp.zeros((hx_rows, ny), jnp.float32)
-
-    def coarse_neighbours(k, below, f, above):
-        cx, cy = cof[k, 2], cof[k, 3]
-        zl = jnp.where(even, pltpu.roll(below, ny - 1, 1), pltpu.roll(f, 1, 1))
-        zh = jnp.where(even, pltpu.roll(f, ny - 1, 1), pltpu.roll(above, 1, 1))
-        total = cx * pltpu.roll(f, 1, 0)
-        total = total + pltpu.roll(cx * f, hx_rows - 1, 0)
-        total = total + cy * pltpu.roll(f, 2, 1)
-        total = total + pltpu.roll(cy * f, ny - 2, 1)
-        return total + cof[k, 0] * zl + cof[k, 4] * zh
-
-    def coarse_sweep(fields):
-        swept = []
-        for k in range(3):
-            total = coarse_neighbours(k, fields[k], fields[k + 1], fields[k + 2])
-            swept.append((1.0 - OMEGA) * fields[k + 1] + cof[k, 1] * (b1[k] + total))
-        return [zero] + swept + [zero]
-
-    v1 = [zero] + [cof[k, 1] * b1[k] for k in range(3)] + [zero]
-    v2 = coarse_sweep(v1)
-    own_total = coarse_neighbours(1, v2[1], v2[2], v2[3])
-    r1 = jnp.where(cof[1, 1] > 0.0, b1[1] - d1[...] * v2[2] + own_total, 0.0)
-    gather(row_out, row_all, 1, (plane_sums(r1),))
-    vn[1] = (1.0 - OMEGA) * v2[2] + cof[1, 1] * (b1[1] + own_total)
-    send(vn_up, vn_low)
-
-    parts = []
-    for k in range(3):
-        weight, cx, cy = cof[k, 1], cof[k, 2], cof[k, 3]
-        around = cx + pltpu.roll(cx, hx_rows - 1, 0) + cy + pltpu.roll(cy, ny - 2, 1)
-        own_part = jnp.where(weight > 0.0, 1.0 - OMEGA, 0.0) + weight * around
-        parts.append((own_part, weight * cof[k, 0], weight * cof[k, 4]))
     receive(vn_up, vn_low)
-
     gather_wait(row_all, 1, 1, 1)
     be, bo = line_rows(row_all, 0)
     reduced = be + to_low * back(bo, 1) + to_up * bo
@@ -426,6 +456,7 @@
             pltpu.SemaphoreType.DMA((3,)),
             pltpu.SemaphoreType.DMA((2, 16)),
             pltpu.SemaphoreType.DMA((2, 2)),
+            pltpu.SemaphoreType.REGULAR((n.bit_length(),)),
         ],
         compiler_params=pltpu.CompilerParams(collective_id=0, has_side_effects=True),
     )(rhs, labels, sigma_table.T)

time: 24.2 us -> 23.6 us (0.975)
  Pallas kernels: 23.4 us -> 22.8 us
    pallas_call x1, Pallas kernels: 23.4 us -> 22.8 us  [on_device(): pl.pallas_call(functools.partial(kernel, n), out_shape=pltpu.VMEM(rhs.sha...]
where the time goes in v4:
time: 23.6 us; the launch traced here: 23.5 us
  Pallas kernels  22.8 us (97%)
  local copies, waits for them, and re-layouts  0.71 us (3%)
    pallas_call x1, Pallas kernels, on_device(): pl.pallas_call(functools.partial(kernel, n), out_shape=pltpu.VMEM(rhs.sha...  22.8 us
    unnamed x1, local copies, waits for them, and re-layouts  0.71 us

profile of v4, /device:TPU:0, one launch (start us, length us, event | category | flops | bytes accessed | tf_op | source)
XLA Modules:
  0.0 23.5 jit_solution(1775230337779979451)
XLA Ops:
  0.0 22.8 %shard_map.37 = f32[1,4,128,128]{3,2,1,0:T(8,128)S(1)} custom-call(f32[1,4,128,128]{3,2,1,0:T(8,128)} %rhs_hbm.1, s32[4,128,128]{2,1,0:T(8,128)} %lab_hbm.1, f32[3,5]{1,0:T(4,128)} %bitcast.1), custom_call_target="tpu_custom_call" | custom-call | tf_op jit(solution)/shard_map/pallas_call | solution.py:439
  22.8 0.7 %copy.5 = f32[1,4,128,128]{3,2,1,0:T(8,128)} copy(f32[1,4,128,128]{3,2,1,0:T(8,128)S(1)} %shard_map.37) | data formatting | bytes 524288

commit v5 on v4

--- a/solution.py
+++ b/solution.py
@@ -293,11 +293,11 @@
     over(0, 2, lambda k: second_sweep(1 + 5 * k))
     b1[1] = restrict(residual(2) + r3, r4 + residual(5))
     send(b1_up, b1_low)
-    send(u2_up, u2_low)
     for r in range(3, len(rounds)):
         round_end(r)
         round_start(r + 1)
     gather(line_out, line_all, 0, (line_diag, line_face))
+    send(u2_up, u2_low)
 
     receive(cof_up, cof_low)
     cof[0, 4] = jnp.where(even, pltpu.roll(cof[0, 0], ny - 1, 1), pltpu.roll(cof[1, 0], 1, 1))

time: 23.6 us -> 23.6 us (level)
  no operation moved by 1% of the time
where the time goes in v5:
time: 23.6 us; the launch traced here: 23.5 us
  Pallas kernels  22.8 us (97%)
  local copies, waits for them, and re-layouts  0.71 us (3%)
    pallas_call x1, Pallas kernels, on_device(): pl.pallas_call(functools.partial(kernel, n), out_shape=pltpu.VMEM(rhs.sha...  22.8 us
    unnamed x1, local copies, waits for them, and re-layouts  0.71 us

profile of v5, /device:TPU:0, one launch (start us, length us, event | category | flops | bytes accessed | tf_op | source)
XLA Modules:
  0.0 23.5 jit_solution(10447092004447783057)
XLA Ops:
  0.0 22.8 %shard_map.37 = f32[1,4,128,128]{3,2,1,0:T(8,128)S(1)} custom-call(f32[1,4,128,128]{3,2,1,0:T(8,128)} %rhs_hbm.1, s32[4,128,128]{2,1,0:T(8,128)} %lab_hbm.1, f32[3,5]{1,0:T(4,128)} %bitcast.1), custom_call_target="tpu_custom_call" | custom-call | tf_op jit(solution)/shard_map/pallas_call | solution.py:439
  22.8 0.7 %copy.5 = f32[1,4,128,128]{3,2,1,0:T(8,128)} copy(f32[1,4,128,128]{3,2,1,0:T(8,128)S(1)} %shard_map.37) | data formatting | bytes 524288
